TPU v7x, 32 devices: a whole 2x2x4 slice. The times are simulated.
32 devices in a mesh: scen: 8 (over z, core), dec: 4 (over y, x).
Axes of the slice: x: 2, y: 2, z: 4, core: 2. Of those that a mesh axis runs over, the one named last changes fastest.
Arguments:
- order_qty: bfloat16 [8192, 4096], P('dec', 'scen'), may hold values from 0 to 2
- multiplier: float32 [8192, 4096], P('dec', 'scen'), may hold values from -6 to 6
- unit_cost: bfloat16 [8192, 4096], P('dec', 'scen'), may hold values from -6 to 6
- demand: bfloat16 [2048, 4096], P('dec', 'scen'), may hold values from -6 to 6
- technology: bfloat16 [8192, 2048], P('dec'), may hold values from -0.0625 to 0.0625
- kkt_inverse: bfloat16 [2048, 2048], P('dec'), may hold values from -1 to 3
- probability: float32 [4096], P('scen'), may hold values from 0.1 to 1
- scenario_node: int32 [4096, 1], P('scen'), may hold values from 0 to 511
Outputs:
- planned: bfloat16 [8192, 4096], P('dec', 'scen')
- recourse: bfloat16 [2048, 4096], P('dec', 'scen')
- consensus: float32 [8192, 512], P('dec')
- multiplier_next: float32 [8192, 4096], P('dec', 'scen')
Inputs may be any that keep to these rules, and one draw needn't show every extreme that they name: `scenario_node`: every one of the 512 nodes is the node of some scenario.
All inputs are finite; a program needn't handle non-finite values.
Results may differ from a plain program's by a relative error of at most 0.023.
Values may be sent and summed in bfloat16 or wider, within the bound.
No kernel may reach another device: no remote copies, remote signals or barrier semaphores. Data moves between devices by JAX's collectives and lax.ppermute only.
A program may use at most 128 MiB of HBM per device.

v0:
```python
import jax
import jax.numpy as jnp
from jax import lax
from jax.sharding import PartitionSpec as P

G = 512
step_size = 0.5
penalty = 2.0


def on_device(
    order_qty, multiplier, unit_cost, demand, technology, kkt_inverse, probability, scenario_node
):
    contract_first = (((0,), (0,)), ((), ()))
    columns = technology
    supply = lax.psum_scatter(
        lax.dot_general(columns, order_qty, contract_first, preferred_element_type=jnp.float32),
        "dec",
        scatter_dimension=0,
        tiled=True,
    )
    right_side = (demand.astype(jnp.float32) - supply).astype(jnp.bfloat16)
    columns = kkt_inverse
    solved = jnp.dot(
        columns,
        lax.all_gather(right_side, "dec", axis=0, tiled=True),
        preferred_element_type=jnp.float32,
    )
    recourse = solved.astype(jnp.bfloat16)
    columns = technology
    linked = jnp.dot(
        columns,
        lax.all_gather(recourse, "dec", axis=0, tiled=True),
        preferred_element_type=jnp.float32,
    )
    gradient = unit_cost.astype(jnp.float32) + multiplier + linked
    planned = jnp.maximum(order_qty.astype(jnp.float32) - step_size * gradient, 0.0).astype(
        jnp.bfloat16
    )
    node_list = scenario_node[:, 0]
    node_ids = jnp.arange(G, dtype=jnp.int32)
    member = (node_list[:, None] == node_ids[None, :]).astype(jnp.float32)
    weight_table = member * probability[:, None]
    weight_high = weight_table.astype(jnp.bfloat16)
    weight_low = (weight_table - weight_high.astype(jnp.float32)).astype(jnp.bfloat16)
    totals = jnp.dot(planned, weight_high, preferred_element_type=jnp.float32)
    totals = totals + jnp.dot(planned, weight_low, preferred_element_type=jnp.float32)
    masses = jnp.dot(probability, member, precision=lax.Precision.HIGHEST)
    totals, masses = (
        lax.psum(totals.astype(jnp.bfloat16), "scen").astype(jnp.float32),
        lax.psum(masses.astype(jnp.bfloat16), "scen").astype(jnp.float32),
    )
    consensus = totals / masses[None, :]
    spread_back = jnp.take(consensus, node_list, axis=1)
    multiplier_next = multiplier + penalty * (planned.astype(jnp.float32) - spread_back)
    return (planned, recourse, consensus, multiplier_next)


def solution(mesh):
    placed = (
        P("dec", "scen"),
        P("dec", "scen"),
        P("dec", "scen"),
        P("dec", "scen"),
        P("dec", None),
        P("dec", None),
        P("scen"),
        P("scen", None),
    )
    return jax.shard_map(
        on_device,
        mesh=mesh,
        in_specs=placed,
        out_specs=(P("dec", "scen"), P("dec", "scen"), P("dec", None), P("dec", "scen")),
        check_vma=False,
    )
```

profile of v0, /device:TPU:0, one launch (start us, length us, event | category | flops | bytes accessed | tf_op | source)
XLA Modules:
  0.0 267.7 jit_solution(8834524278029128329)
XLA Ops:
  7.2 0.0 copy-start
  7.2 0.0 reduce-scatter.2.cloned.1.call-start
  7.2 10.7 %fusion.20 = f32[2048,512]{1,0:T(8,128)} fusion(bf16[2048,2048]{1,0:T(8,128)(2,1)} %param.12, bf16[2048,512]{1,0:T(8,128)(2,1)} %param.8), kind=kOutput, calls=%fused_computation.32 | convolution fusion | flops 4294967296 | bytes 14680064 | tf_op jit(solution)/shard_map/dot_general | solution.py:17
  17.9 0.0 copy-start.5
  17.9 0.0 reduce-scatter.2.cloned.1.call-update
  17.9 0.0 all-gather.3.cloned.1.call-start
  18.0 55.5 %reduce-scatter.2.cloned.1.call-done = f32[512,512]{1,0:T(8,128)} async-done(((f32[2048,512]{1,0:T(8,128)}), f32[512,512]{1,0:T(8,128)}) %reduce-scatter.2.cloned.1.call-update) | async-done | bytes 1048592 | tf_op jit(solution)/shard_map/reduce_scatter | solution.py:16
  73.4 0.0 copy-done.5
  73.4 2.2 subtract_convert_fusion
  75.6 0.0 all-gather.3.cloned.1.call-update
  75.7 0.0 all-gather.5.cloned.1.call-start
  75.7 35.4 %all-gather.3.cloned.1.call-done = bf16[2048,512]{1,0:T(8,128)(2,1)} async-done(((bf16[512,512]{1,0:T(8,128)(2,1)}), bf16[2048,512]{1,0:T(8,128)(2,1)}) %all-gather.3.cloned.1.call-update) | async-done | bytes 2097168 | tf_op jit(solution)/shard_map/all_gather | solution.py:26
  111.1 0.0 copy-done
  111.1 3.7 %fusion.6 = bf16[512,512]{0,1:T(8,128)(2,1)} fusion(bf16[2048,512]{1,0:T(8,128)(2,1)} %all-gather.3.cloned.1.call-done, bf16[512,2048]{1,0:T(8,128)(2,1)S(1)} %copy-done), kind=kOutput, calls=%fused_computation.14 | convolution fusion | flops 1074003968 | bytes 4718592 | tf_op jit(solution)/shard_map/dot_general | solution.py:24
  114.7 0.0 all-gather.5.cloned.1.call-update
  114.8 0.2 all-reduce.2.cloned.1.call-start
  115.0 3.9 %copy.12 = bf16[2048,512]{0,1:T(8,128)(2,1)} copy(bf16[2048,512]{1,0:T(8,128)(2,1)} %param.8) | data formatting | bytes 4194304 | tf_op args[0]
  118.9 0.0 copy-start.3
  118.9 5.6 %copy.14 = f32[2048,512]{0,1:T(8,128)} copy(f32[2048,512]{1,0:T(8,128)} %param.9) | data formatting | bytes 8388608 | tf_op args[1]
  124.5 0.0 copy-done.3
  124.5 2.4 copy.13
  126.8 0.0 copy-start.6
  126.8 0.0 copy-start.7
  126.9 23.1 %all-gather.5.cloned.1.call-done = bf16[2048,512]{0,1:T(8,128)(2,1)} async-done(((bf16[512,512]{0,1:T(8,128)(2,1)}), bf16[2048,512]{0,1:T(8,128)(2,1)}) %all-gather.5.cloned.1.call-update) | async-done | bytes 2097168 | tf_op jit(solution)/shard_map/all_gather | solution.py:33
  150.0 11.3 %fusion.5 = bf16[2048,512]{0,1:T(8,128)(2,1)S(1)} fusion(f32[2048,512]{0,1:T(8,128)} %copy.14, bf16[2048,512]{0,1:T(8,128)(2,1)} %copy.13, bf16[2048,512]{0,1:T(8,128)(2,1)} %copy.12, bf16[2048,512]{0,1:T(8,128)(2,1)} %all-gather.5.cloned.1.call-done, bf16[2048,2048]{1,0:T(8,128)(2,1)} %param.12), kind=kOutput, calls=%fused_computation.8 | convolution fusion | flops 4303355904 | bytes 20971520 | tf_op jit(solution)/shard_map/dot_general | solution.py:31
  161.3 0.0 copy-start.2
  161.3 0.0 copy-done.6
  161.3 0.0 copy-done.7
  161.3 1.4 fusion.9
  162.7 0.0 copy-start.4
  162.7 2.8 %add_convert_fusion = bf16[2048,512]{1,0:T(8,128)(2,1)} fusion(f32[2048,512]{1,0:T(8,128)S(1)} %fusion.9, bf16[2048,512]{0,1:T(8,128)(2,1)S(1)} %fusion.5, f32[512]{0:T(512)S(1)} %copy-done.7, s32[512]{0:T(512)S(1)} %bitcast.33), kind=kOutput, calls=%fused_computation.10 | convolution fusion | flops 1077411840 | bytes 8392704 | tf_op jit(solution)/shard_map/dot_general | solution.py:47
  165.5 0.0 all-reduce.2.cloned.1.call-update
  165.6 0.5 fusion.8
  166.1 16.8 %psum.15 = bf16[512]{0:T(512)(128)(2,1)S(1)} all-reduce(bf16[512]{0:T(512)(128)(2,1)S(1)} %convert_element_type.58), channel_id=1, replica_groups=mesh['scen'=8,'dec'=4] {'scen'}, use_global_device_ids=true, to_apply=%region_2.0 | all-reduce | flops 512 | bytes 2048 | tf_op jit(solution)/shard_map/psum | solution.py:51
  182.9 0.0 copy-done.4
  182.9 1.0 copy.18
  184.0 0.0 copy-done.2
  184.0 2.5 copy.17
  186.4 44.3 %all-reduce.2.cloned.1.call-done = bf16[2048,512]{1,0:T(8,128)(2,1)} async-done(((bf16[2048,512]{1,0:T(8,128)(2,1)}), bf16[2048,512]{1,0:T(8,128)(2,1)}) %all-reduce.2.cloned.1.call-update) | async-done | bytes 2097168 | tf_op jit(solution)/shard_map/psum | solution.py:50
  230.8 4.2 %convert_divide_fusion = f32[2048,512]{1,0:T(8,128)} fusion(bf16[2048,512]{1,0:T(8,128)(2,1)} %all-reduce.2.cloned.1.call-done, f32[512]{0:T(512)S(1)} %convert_element_type.59), kind=kLoop, calls=%fused_computation.9 | loop fusion | flops 2097152 | bytes 6293504 | tf_op jit(solution)/shard_map/div | solution.py:53
  235.0 5.5 %copy.15 = f32[2048,512]{0,1:T(8,128)} copy(f32[2048,512]{1,0:T(8,128)} %convert_divide_fusion) | data formatting | bytes 8388608 | tf_op jit(solution)/shard_map/div | solution.py:53
  240.5 7.6 %gather_fusion = f32[512,2048]{1,0:T(8,128)} fusion(f32[2048,512]{0,1:T(8,128)} %copy.15, s32[1024]{0:T(1024)S(1)} %pad_clamp_fusion), kind=kCustom, calls=%fused_computation | custom fusion | bytes 8390656 | tf_op jit(solution)/shard_map/jit(_take)/gather | solution.py:54
  248.1 0.0 copy-start.1
  248.1 7.7 %fusion.1 = f32[2048,512]{0,1:T(8,128)} fusion(f32[2048,512]{0,1:T(8,128)} %copy.14, f32[512,2048]{1,0:T(8,128)} %gather_fusion, bf16[2048,512]{0,1:T(8,128)(2,1)} %copy-done.2, pred[512]{0:T(512)(128)(4,1)S(1)} %get-tuple-element.8), kind=kLoop, calls=%fused_computation.3 | loop fusion | flops 5242880 | bytes 14680576 | tf_op jit(solution)/shard_map/add | solution.py:55
  255.8 5.3 %copy.19 = f32[2048,512]{1,0:T(8,128)} copy(f32[2048,512]{0,1:T(8,128)} %fusion.1) | data formatting | bytes 8388608
  261.1 0.0 copy-done.1
  (4 shorter events, 0.0 us)
Async XLA Ops:
  7.2 103.9 %copy-start = (bf16[512,2048]{1,0:T(8,128)(2,1)S(1)}, bf16[512,2048]{1,0:T(8,128)(2,1)}, u32[]{:S(2)}) copy-start(bf16[512,2048]{1,0:T(8,128)(2,1)} %param.13) | copy-start | bytes 6291460
  7.2 66.3 %reduce-scatter.2.cloned.1.call-start = ((), (), s32[]{:S(2)}) async-start(), calls=%async_computation.1 | async-start | bytes 5242880 | tf_op jit(solution)/shard_map/reduce_scatter | solution.py:16
  17.9 55.5 %copy-start.5 = (bf16[512,512]{1,0:T(8,128)(2,1)S(1)}, bf16[512,512]{1,0:T(8,128)(2,1)}, u32[]{:S(2)}) copy-start(bf16[512,512]{1,0:T(8,128)(2,1)} %param.11) | copy-start | bytes 1572868
  17.9 93.1 %all-gather.3.cloned.1.call-start = ((), (), s32[]{:S(2)}) async-start(), calls=%async_computation.2 | async-start | bytes 2621440 | tf_op jit(solution)/shard_map/all_gather | solution.py:26
  75.7 74.3 %all-gather.5.cloned.1.call-start = ((), (), s32[]{:S(2)}) async-start(), calls=%async_computation.3 | async-start | bytes 2621440 | tf_op jit(solution)/shard_map/all_gather | solution.py:33
  114.8 116.0 %all-reduce.2.cloned.1.call-start = ((), (), s32[]{:S(2)}) async-start(), calls=%async_computation.4 | async-start | bytes 4194304 | tf_op jit(solution)/shard_map/psum | solution.py:50
  118.9 5.6 %copy-start.3 = (bf16[2048,512]{1,0:T(8,128)(2,1)S(1)}, bf16[2048,512]{1,0:T(8,128)(2,1)}, u32[]{:S(2)}) copy-start(bf16[2048,512]{1,0:T(8,128)(2,1)} %param.10) | copy-start | bytes 6291460
  126.8 34.5 %copy-start.6 = (s32[512,1]{0,1:T(1,128)S(1)}, s32[512,1]{0,1:T(1,128)}, u32[]{:S(2)}) copy-start(s32[512,1]{0,1:T(1,128)} %param.15) | copy-start | bytes 6148
  126.8 34.5 %copy-start.7 = (f32[512]{0:T(512)S(1)}, f32[512]{0:T(512)}, u32[]{:S(2)}) copy-start(f32[512]{0:T(512)} %param.14) | copy-start | bytes 6148
  161.3 22.6 %copy-start.2 = (bf16[2048,512]{0,1:T(8,128)(2,1)}, bf16[2048,512]{0,1:T(8,128)(2,1)S(1)}, u32[]{:S(2)}) copy-start(bf16[2048,512]{0,1:T(8,128)(2,1)S(1)} %fusion.5) | copy-start | bytes 6291460
  162.7 20.2 %copy-start.4 = (bf16[512,512]{0,1:T(8,128)(2,1)S(1)}, bf16[512,512]{0,1:T(8,128)(2,1)}, u32[]{:S(2)}) copy-start(bf16[512,512]{0,1:T(8,128)(2,1)} %fusion.6) | copy-start | bytes 1572868
  248.1 13.0 %copy-start.1 = (bf16[512,2048]{1,0:T(8,128)(2,1)S(1)}, bf16[512,2048]{1,0:T(8,128)(2,1)}, u32[]{:S(2)}) copy-start(bf16[512,2048]{1,0:T(8,128)(2,1)} %param.13) | copy-start | bytes 6291460
Sparse Core Ops, SparseCore 0:
  18.1 55.3 reduce-scatter.1
  75.9 35.1 all-gather.2
  114.9 35.0 all-gather.4
  165.7 65.0 all-reduce.1
where the time goes:
time: 268 us
  waiting for transfers between devices  158 us (59%)
  local copies, waits for them, and re-layouts  33.8 us (13%)
  matrix products  30.4 us (11%)
  blocking collectives  16.8 us (6%)
  other arithmetic  14.1 us (5%)
  between operations  13.8 us (5%)
    reduce_scatter x1, waiting for transfers between devices, on_device(): lax.psum_scatter(lax.dot_general(columns, order_qty, contract_first, pref...  55.5 us
    psum x1, waiting for transfers between devices, on_device(): lax.psum(totals.astype(jnp.bfloat16), 'scen').astype(jnp.float32)  44.3 us
    all_gather x1, waiting for transfers between devices, on_device(): lax.all_gather(right_side, 'dec', axis=0, tiled=True)  35.4 us
    all_gather x1, waiting for transfers between devices, on_device(): lax.all_gather(recourse, 'dec', axis=0, tiled=True)  23.1 us
    unnamed x22, local copies, waits for them, and re-layouts  20.7 us
    psum x1, blocking collectives, on_device(): lax.psum(masses.astype(jnp.bfloat16), 'scen').astype(jnp.float32)  16.8 us
    dot_general x1, matrix products, on_device(): jnp.dot(columns, lax.all_gather(recourse, 'dec', axis=0, tiled=True), pre...  11.3 us
    dot_general x1, matrix products, on_device(): lax.dot_general(columns, order_qty, contract_first, preferred_element_typ...  10.7 us
  transfers between devices with their start and end apart: 4, of which 4 were waited for; matrix products, arithmetic and copies ran while one was open for 6% of the time, Pallas kernels for 0%

commit v1 on v0

--- a/solution.py
+++ b/solution.py
@@ -47,7 +47,7 @@
     totals = totals + jnp.dot(planned, weight_low, preferred_element_type=jnp.float32)
     masses = jnp.dot(probability, member, precision=lax.Precision.HIGHEST)
     totals, masses = (
-        lax.psum(totals.astype(jnp.bfloat16), "scen").astype(jnp.float32),
+        jnp.sum(lax.all_gather(totals.astype(jnp.bfloat16), "scen"), axis=0).astype(jnp.float32),
         lax.psum(masses.astype(jnp.bfloat16), "scen").astype(jnp.float32),
     )
     consensus = totals / masses[None, :]

time: 268 us -> 366 us (1.37)
  waiting for transfers between devices: 158 us -> 244 us
  other arithmetic: 14.1 us -> 23 us
    all_gather x0 -> x1, waiting for transfers between devices: none -> 130 us  [on_device(): lax.all_gather(totals.astype(jnp.bfloat16), 'scen')]
    psum x1 -> x0, waiting for transfers between devices: 44.3 us -> none  [on_device(): lax.psum(totals.astype(jnp.bfloat16), 'scen').astype(jnp.float32)]
    reduce_sum x0 -> x1, other arithmetic: none -> 10.5 us  [on_device(): jnp.sum(lax.all_gather(totals.astype(jnp.bfloat16), 'scen'), axis=0)]
    div x1 -> x0, local copies, waits for them, and re-layouts: 5.46 us -> none  [on_device(): consensus = totals / masses[None, :]]
    unnamed x22 -> x23, local copies, waits for them, and re-layouts: 20.7 us -> 26.1 us
  transfers between devices with their start and end apart: 4 -> 4, of which waited for: 4 -> 4; matrix products, arithmetic and copies ran while one was open for 6% -> 4% of each run, Pallas kernels for 0% -> 0%
where the time goes in v1:
time: 366 us; the launch traced here: 365 us
  waiting for transfers between devices  244 us (67%)
  local copies, waits for them, and re-layouts  36.6 us (10%)
  matrix products  30.4 us (8%)
  other arithmetic  23 us (6%)
  blocking collectives  17 us (5%)
  between operations  13.9 us (4%)
    all_gather x1, waiting for transfers between devices, on_device(): lax.all_gather(totals.astype(jnp.bfloat16), 'scen')  130 us
    reduce_scatter x1, waiting for transfers between devices, on_device(): lax.psum_scatter(lax.dot_general(columns, order_qty, contract_first, pref...  55.5 us
    all_gather x1, waiting for transfers between devices, on_device(): lax.all_gather(right_side, 'dec', axis=0, tiled=True)  35.4 us
    unnamed x23, local copies, waits for them, and re-layouts  26.1 us
    all_gather x1, waiting for transfers between devices, on_device(): lax.all_gather(recourse, 'dec', axis=0, tiled=True)  23.1 us
    psum x1, blocking collectives, on_device(): lax.psum(masses.astype(jnp.bfloat16), 'scen').astype(jnp.float32)  17 us
    dot_general x1, matrix products, on_device(): jnp.dot(columns, lax.all_gather(recourse, 'dec', axis=0, tiled=True), pre...  11.3 us
    dot_general x1, matrix products, on_device(): lax.dot_general(columns, order_qty, contract_first, preferred_element_typ...  10.7 us
  transfers between devices with their start and end apart: 4, of which 4 were waited for; matrix products, arithmetic and copies ran while one was open for 4% of the time, Pallas kernels for 0%

profile of v1, /device:TPU:0, one launch (start us, length us, event | category | flops | bytes accessed | tf_op | source)
XLA Modules:
  0.0 365.4 jit_solution(17045630498027555449)
XLA Ops:
  7.2 0.0 copy-start
  7.2 0.0 reduce-scatter.2.cloned.1.call-start
  7.2 10.7 %fusion.20 = f32[2048,512]{1,0:T(8,128)} fusion(bf16[2048,2048]{1,0:T(8,128)(2,1)} %param.12, bf16[2048,512]{1,0:T(8,128)(2,1)} %param.8), kind=kOutput, calls=%fused_computation.32 | convolution fusion | flops 4294967296 | bytes 14680064 | tf_op jit(solution)/shard_map/dot_general | solution.py:17
  17.9 0.0 copy-start.5
  17.9 0.0 reduce-scatter.2.cloned.1.call-update
  17.9 0.0 all-gather.5.cloned.1.call-start
  18.0 55.5 %reduce-scatter.2.cloned.1.call-done = f32[512,512]{1,0:T(8,128)} async-done(((f32[2048,512]{1,0:T(8,128)}), f32[512,512]{1,0:T(8,128)}) %reduce-scatter.2.cloned.1.call-update) | async-done | bytes 1048592 | tf_op jit(solution)/shard_map/reduce_scatter | solution.py:16
  73.4 0.0 copy-done.5
  73.4 2.2 subtract_convert_fusion
  75.6 0.0 all-gather.5.cloned.1.call-update
  75.7 0.0 all-gather.7.cloned.1.call-start
  75.7 35.4 %all-gather.5.cloned.1.call-done = bf16[2048,512]{1,0:T(8,128)(2,1)} async-done(((bf16[512,512]{1,0:T(8,128)(2,1)}), bf16[2048,512]{1,0:T(8,128)(2,1)}) %all-gather.5.cloned.1.call-update) | async-done | bytes 2097168 | tf_op jit(solution)/shard_map/all_gather | solution.py:26
  111.1 0.0 copy-done
  111.1 3.7 %fusion.6 = bf16[512,512]{0,1:T(8,128)(2,1)} fusion(bf16[2048,512]{1,0:T(8,128)(2,1)} %all-gather.5.cloned.1.call-done, bf16[512,2048]{1,0:T(8,128)(2,1)S(1)} %copy-done), kind=kOutput, calls=%fused_computation.14 | convolution fusion | flops 1074003968 | bytes 4718592 | tf_op jit(solution)/shard_map/dot_general | solution.py:24
  114.7 0.0 all-gather.7.cloned.1.call-update
  114.8 0.2 all-gather.9.cloned.1.call-start
  115.0 3.9 %copy.20 = bf16[2048,512]{0,1:T(8,128)(2,1)} copy(bf16[2048,512]{1,0:T(8,128)(2,1)} %param.8) | data formatting | bytes 4194304 | tf_op args[0]
  118.9 0.0 copy-start.3
  118.9 5.6 %copy.22 = f32[2048,512]{0,1:T(8,128)} copy(f32[2048,512]{1,0:T(8,128)} %param.9) | data formatting | bytes 8388608 | tf_op args[1]
  124.5 0.0 copy-done.3
  124.5 2.4 copy.21
  126.8 0.0 copy-start.6
  126.8 0.0 copy-start.7
  126.9 23.1 %all-gather.7.cloned.1.call-done = bf16[2048,512]{0,1:T(8,128)(2,1)} async-done(((bf16[512,512]{0,1:T(8,128)(2,1)}), bf16[2048,512]{0,1:T(8,128)(2,1)}) %all-gather.7.cloned.1.call-update) | async-done | bytes 2097168 | tf_op jit(solution)/shard_map/all_gather | solution.py:33
  150.0 11.3 %fusion.5 = bf16[2048,512]{0,1:T(8,128)(2,1)S(1)} fusion(f32[2048,512]{0,1:T(8,128)} %copy.22, bf16[2048,512]{0,1:T(8,128)(2,1)} %copy.21, bf16[2048,512]{0,1:T(8,128)(2,1)} %copy.20, bf16[2048,512]{0,1:T(8,128)(2,1)} %all-gather.7.cloned.1.call-done, bf16[2048,2048]{1,0:T(8,128)(2,1)} %param.12), kind=kOutput, calls=%fused_computation.8 | convolution fusion | flops 4303355904 | bytes 20971520 | tf_op jit(solution)/shard_map/dot_general | solution.py:31
  161.3 0.0 copy-start.2
  161.3 0.0 copy-done.6
  161.3 0.0 copy-done.7
  161.3 1.4 fusion.9
  162.7 0.0 copy-start.4
  162.7 2.8 add_convert_fusion
  165.5 0.0 all-gather.9.cloned.1.call-update
  165.6 0.5 fusion.8
  166.1 17.0 %psum.7 = bf16[512]{0:T(512)(128)(2,1)S(1)} all-reduce(bf16[512]{0:T(512)(128)(2,1)S(1)} %convert_element_type.60), channel_id=1, replica_groups=mesh['scen'=8,'dec'=4] {'scen'}, use_global_device_ids=true, to_apply=%region_2.0 | all-reduce | flops 512 | bytes 2048 | tf_op jit(solution)/shard_map/psum | solution.py:51
  183.1 0.0 copy-done.4
  183.1 1.0 copy.26
  184.1 0.0 copy-done.2
  184.1 2.5 copy.25
  186.6 130.3 %all-gather.9.cloned.1.call-done = bf16[16384,512]{1,0:T(8,128)(2,1)} async-done(((bf16[2048,512]{1,0:T(8,128)(2,1)}), bf16[16384,512]{1,0:T(8,128)(2,1)}) %all-gather.9.cloned.1.call-update) | async-done | bytes 16777232 | tf_op jit(solution)/shard_map/all_gather | solution.py:50
  316.8 10.5 %reduce_sum.12 = bf16[2048,512]{1,0:T(8,128)(2,1)} reduce(bf16[8,2048,512]{2,1,0:T(8,128)(2,1)} %bitcast.32, bf16[]{:T(256)} %constant.20.clone.1), dimensions={0}, to_apply=%region_1.0 | reduce | flops 7340032 | bytes 18874370 | tf_op jit(solution)/shard_map/reduce_sum | solution.py:50
  327.4 2.9 copy.23
  330.3 2.5 convert_divide_fusion
  332.8 5.3 %copy.27 = f32[2048,512]{1,0:T(8,128)} copy(f32[2048,512]{0,1:T(8,128)} %convert_divide_fusion) | data formatting | bytes 8388608
  338.2 7.6 %gather_fusion = f32[512,2048]{1,0:T(8,128)} fusion(f32[2048,512]{0,1:T(8,128)} %convert_divide_fusion, s32[1024]{0:T(1024)S(1)} %pad_clamp_fusion), kind=kCustom, calls=%fused_computation | custom fusion | bytes 8390656 | tf_op jit(solution)/shard_map/jit(_take)/gather | solution.py:54
  345.8 0.0 copy-start.1
  345.8 7.7 %fusion.1 = f32[2048,512]{0,1:T(8,128)} fusion(f32[2048,512]{0,1:T(8,128)} %copy.22, f32[512,2048]{1,0:T(8,128)} %gather_fusion, bf16[2048,512]{0,1:T(8,128)(2,1)} %copy-done.2, pred[512]{0:T(512)(128)(4,1)S(1)} %get-tuple-element.12), kind=kLoop, calls=%fused_computation.3 | loop fusion | flops 5242880 | bytes 14680576 | tf_op jit(solution)/shard_map/add | solution.py:55
  353.5 5.3 %copy.28 = f32[2048,512]{1,0:T(8,128)} copy(f32[2048,512]{0,1:T(8,128)} %fusion.1) | data formatting | bytes 8388608
  358.8 0.0 copy-done.1
  (4 shorter events, 0.0 us)
Async XLA Ops:
  7.2 103.9 %copy-start = (bf16[512,2048]{1,0:T(8,128)(2,1)S(1)}, bf16[512,2048]{1,0:T(8,128)(2,1)}, u32[]{:S(2)}) copy-start(bf16[512,2048]{1,0:T(8,128)(2,1)} %param.13) | copy-start | bytes 6291460
  7.2 66.3 %reduce-scatter.2.cloned.1.call-start = ((), (), s32[]{:S(2)}) async-start(), calls=%async_computation.1 | async-start | bytes 5242880 | tf_op jit(solution)/shard_map/reduce_scatter | solution.py:16
  17.9 55.5 %copy-start.5 = (bf16[512,512]{1,0:T(8,128)(2,1)S(1)}, bf16[512,512]{1,0:T(8,128)(2,1)}, u32[]{:S(2)}) copy-start(bf16[512,512]{1,0:T(8,128)(2,1)} %param.11) | copy-start | bytes 1572868
  17.9 93.1 %all-gather.5.cloned.1.call-start = ((), (), s32[]{:S(2)}) async-start(), calls=%async_computation.2 | async-start | bytes 2621440 | tf_op jit(solution)/shard_map/all_gather | solution.py:26
  75.7 74.3 %all-gather.7.cloned.1.call-start = ((), (), s32[]{:S(2)}) async-start(), calls=%async_computation.3 | async-start | bytes 2621440 | tf_op jit(solution)/shard_map/all_gather | solution.py:33
  114.8 202.1 %all-gather.9.cloned.1.call-start = ((), (), s32[]{:S(2)}) async-start(), calls=%async_computation.4 | async-start | bytes 18874368 | tf_op jit(solution)/shard_map/all_gather | solution.py:50
  118.9 5.6 %copy-start.3 = (bf16[2048,512]{1,0:T(8,128)(2,1)S(1)}, bf16[2048,512]{1,0:T(8,128)(2,1)}, u32[]{:S(2)}) copy-start(bf16[2048,512]{1,0:T(8,128)(2,1)} %param.10) | copy-start | bytes 6291460
  126.8 34.5 %copy-start.6 = (s32[512,1]{0,1:T(1,128)S(1)}, s32[512,1]{0,1:T(1,128)}, u32[]{:S(2)}) copy-start(s32[512,1]{0,1:T(1,128)} %param.15) | copy-start | bytes 6148
  126.8 34.5 %copy-start.7 = (f32[512]{0:T(512)S(1)}, f32[512]{0:T(512)}, u32[]{:S(2)}) copy-start(f32[512]{0:T(512)} %param.14) | copy-start | bytes 6148
  161.3 22.8 %copy-start.2 = (bf16[2048,512]{0,1:T(8,128)(2,1)}, bf16[2048,512]{0,1:T(8,128)(2,1)S(1)}, u32[]{:S(2)}) copy-start(bf16[2048,512]{0,1:T(8,128)(2,1)S(1)} %fusion.5) | copy-start | bytes 6291460
  162.7 20.3 %copy-start.4 = (bf16[512,512]{0,1:T(8,128)(2,1)S(1)}, bf16[512,512]{0,1:T(8,128)(2,1)}, u32[]{:S(2)}) copy-start(bf16[512,512]{0,1:T(8,128)(2,1)} %fusion.6) | copy-start | bytes 1572868
  345.8 13.0 %copy-start.1 = (bf16[512,2048]{1,0:T(8,128)(2,1)S(1)}, bf16[512,2048]{1,0:T(8,128)(2,1)}, u32[]{:S(2)}) copy-start(bf16[512,2048]{1,0:T(8,128)(2,1)} %param.13) | copy-start | bytes 6291460
Sparse Core Ops, SparseCore 0:
  18.1 55.3 reduce-scatter.1
  75.9 35.1 all-gather.4
  114.9 35.0 all-gather.6
  165.7 151.1 all-gather.8
